TPU v7x, 32 devices: a whole 2x2x4 slice. The times are simulated.
32 devices in a mesh: pair: 2 (over x), grow: 4 (over y, core), gcol: 4 (over z).
Axes of the slice: x: 2, y: 2, z: 4, core: 2. Of those that a mesh axis runs over, the one named last changes fastest.
Arguments:
- core_matrix: bfloat16 [12288, 12288], P('grow', 'gcol'), may hold values from -0.00048828125 to 0.00048828125
- pair_panels: bfloat16 [12, 32, 12288], P('pair', None, ('grow', 'gcol')), may hold values from -6 to 6
- amplitudes: bfloat16 [12, 32, 32], P('pair'), may hold values from -0.1875 to 0.1875
- pair_widths: int32 [12], P('pair'), may hold values from 8 to 32
- batch_plan: int32 [12], P('pair'), may hold values from 0 to 11, each once
Outputs:
- residual: float32 [12, 1024], P('pair', ('grow', 'gcol'))
Inputs may be any that keep to these rules, and one draw needn't show every extreme that they name: batch_plan names every pair exactly once.
All inputs are finite; a program needn't handle non-finite values.
Results may differ from a plain program's by a relative error of at most 0.015.
Values may be sent and summed in bfloat16 or wider, within the bound.
A program may use at most 64 MiB of HBM per device.

v0:
```python
import jax
import jax.numpy as jnp
from jax import lax
from jax.sharding import PartitionSpec as P


def local(core_matrix, pair_panels, amplitudes, pair_widths, batch_plan):
    depth = amplitudes.shape[1]
    live = (
        lax.broadcasted_iota(jnp.int32, (pair_widths.shape[0], depth), 1) < pair_widths[:, None]
    ).astype(jnp.bfloat16)
    masked = amplitudes * live[:, :, None] * live[:, None, :]
    row_index = lax.axis_index("grow")
    col_index = lax.axis_index("gcol")
    row_len = core_matrix.shape[0]
    col_len = core_matrix.shape[1]
    gathered = lax.all_gather(pair_panels, ("grow", "gcol"), axis=2, tiled=True)
    left = lax.dynamic_slice_in_dim(gathered, row_index * row_len, row_len, 2)
    right = lax.dynamic_slice_in_dim(gathered, col_index * col_len, col_len, 2)

    def slot_term(items):
        left_panel, right_panel, amps, mask = items
        projected = jnp.dot(amps, right_panel, preferred_element_type=jnp.float32).astype(
            jnp.bfloat16
        )
        coupled = lax.dot_general(
            left_panel, projected, (((0,), (0,)), ((), ())), preferred_element_type=jnp.float32
        ).astype(jnp.bfloat16)
        coupled = lax.optimization_barrier(coupled)
        weighted = (core_matrix.astype(jnp.float32) * coupled.astype(jnp.float32)).astype(
            jnp.bfloat16
        )
        back = lax.dot_general(
            weighted, right_panel, (((1,), (1,)), ((), ())), preferred_element_type=jnp.float32
        ).astype(jnp.bfloat16)
        partial_sum = jnp.dot(left_panel, back, preferred_element_type=jnp.float32)
        keep = mask.astype(jnp.float32)
        return (partial_sum * keep[:, None] * keep[None, :]).reshape(depth * depth)

    terms = lax.map(slot_term, (left, right, masked, live))
    total = lax.psum(terms, ("grow", "gcol"))
    share = terms.shape[1] // lax.axis_size(("grow", "gcol"))
    reduced = lax.dynamic_slice_in_dim(total, lax.axis_index(("grow", "gcol")) * share, share, 1)
    every_row = lax.all_gather(reduced, "pair", axis=0, tiled=True)
    return jnp.take(every_row, batch_plan, axis=0)


def solution(mesh):
    in_specs = (
        P("grow", "gcol"),
        P("pair", None, ("grow", "gcol")),
        P("pair", None, None),
        P("pair"),
        P("pair"),
    )
    out_specs = P("pair", ("grow", "gcol"))
    return jax.shard_map(local, mesh=mesh, in_specs=in_specs, out_specs=out_specs, check_vma=False)
```

profile of v0, /device:TPU:0, one launch (start us, length us, event | category | flops | bytes accessed | tf_op | source)
XLA Modules:
  0.0 285.3 jit_solution(8804718714653839679)
XLA Ops:
  6.5 0.7 all-gather.3.cloned.1.call-update
  7.3 0.7 compare_select_fusion
  8.0 0.7 compare_and_fusion
  8.6 0.7 fusion.27
  9.3 0.9 multiply_multiply_fusion
  10.2 55.5 %all-gather.3.cloned.1.call-done = bf16[6,32,12288]{2,1,0:T(8,128)(2,1)} async-done(((bf16[6,32,768]{2,1,0:T(8,128)(2,1)}), bf16[6,32,12288]{2,1,0:T(8,128)(2,1)}) %all-gather.3.cloned.1.call-update) | async-done | bytes 4718608 | tf_op jit(solution)/shard_map/all_gather | solution.py:17
  65.8 1.9 constant_dynamic-slice_fusion.1
  67.6 145.8 %while.10 = (s32[]{:T(128)}, f32[6,1024]{1,0:T(8,128)S(1)}, bf16[6,32,3072]{2,1,0:T(8,128)(2,1)S(1)}, bf16[3072,3072]{1,0:T(8,128)(2,1)}, bf16[6,32,32]{2,1,0:T(...) while((s32[]{:T(128)}, f32[6,1024]{1,0:T(8,128)S(1)}, ...), condition=%wide.region_1.2_spmd, body=%wide.region_0.1_spmd.sunk | while | flops 1267927040 | bytes 57442084 | solution.py:40
  67.6 9.3 %convolution_convert_fusion.3 = bf16[3072,3072]{1,0:T(8,128)(2,1)} fusion(bf16[6,32,3072]{2,1,0:T(8,128)(2,1)S(1)} %get-tuple-element.125, s32[]{:T(128)} %get-tuple-element.111, bf16[6,32,3072]{2,1,0:T(8,128)(2,1)S(1)} %get-tuple-element.122, bf16[6,32,32]{2,1,0:T(8,128)(2,1)S(1)} %get-tuple-element.124), kind=kOutput, calls=%fused_computation.3.clone.1 | convolution fusion | flops 619806720 | bytes 19277312 | tf_op jit(solution)/shard_map/while/body/eval_jaxpr/dot_general | solution.py:26
  77.0 14.8 %fusion.41 = f32[32,32]{1,0:T(8,128)S(1)} fusion(bf16[3072,3072]{1,0:T(8,128)(2,1)} %convolution_convert_fusion.3, bf16[3072,3072]{1,0:T(8,128)(2,1)} %get-tuple-element.123, bf16[6,32,3072]{2,1,0:T(8,128)(2,1)S(1)} %get-tuple-element.125, s32[]{:T(128)} %get-tuple-element.111, bf16[6,32,3072]{2,1,0:T(8,128)(2,1)S(1)} %get-tuple-element.122, ...), kind=kOutput, calls=%fused_computation.8.clone.1 | convolution fusion | flops 648120320 | bytes 38148096 | tf_op jit(solution)/shard_map/while/body/eval_jaxpr/dot_general | solution.py:36
  91.8 0.1 broadcast_in_dim.31
  91.8 0.1 dynamic_update_slice.5
  91.9 9.3 %convolution_convert_fusion.3 = bf16[3072,3072]{1,0:T(8,128)(2,1)} fusion(bf16[6,32,3072]{2,1,0:T(8,128)(2,1)S(1)} %get-tuple-element.125, s32[]{:T(128)} %get-tuple-element.111, bf16[6,32,3072]{2,1,0:T(8,128)(2,1)S(1)} %get-tuple-element.122, bf16[6,32,32]{2,1,0:T(8,128)(2,1)S(1)} %get-tuple-element.124), kind=kOutput, calls=%fused_computation.3.clone.1 | convolution fusion | flops 619806720 | bytes 19277312 | tf_op jit(solution)/shard_map/while/body/eval_jaxpr/dot_general | solution.py:26
  101.3 14.8 %fusion.41 = f32[32,32]{1,0:T(8,128)S(1)} fusion(bf16[3072,3072]{1,0:T(8,128)(2,1)} %convolution_convert_fusion.3, bf16[3072,3072]{1,0:T(8,128)(2,1)} %get-tuple-element.123, bf16[6,32,3072]{2,1,0:T(8,128)(2,1)S(1)} %get-tuple-element.125, s32[]{:T(128)} %get-tuple-element.111, bf16[6,32,3072]{2,1,0:T(8,128)(2,1)S(1)} %get-tuple-element.122, ...), kind=kOutput, calls=%fused_computation.8.clone.1 | convolution fusion | flops 648120320 | bytes 38148096 | tf_op jit(solution)/shard_map/while/body/eval_jaxpr/dot_general | solution.py:36
  116.1 0.1 broadcast_in_dim.31
  116.2 9.3 %convolution_convert_fusion.3 = bf16[3072,3072]{1,0:T(8,128)(2,1)} fusion(bf16[6,32,3072]{2,1,0:T(8,128)(2,1)S(1)} %get-tuple-element.125, s32[]{:T(128)} %get-tuple-element.111, bf16[6,32,3072]{2,1,0:T(8,128)(2,1)S(1)} %get-tuple-element.122, bf16[6,32,32]{2,1,0:T(8,128)(2,1)S(1)} %get-tuple-element.124), kind=kOutput, calls=%fused_computation.3.clone.1 | convolution fusion | flops 619806720 | bytes 19277312 | tf_op jit(solution)/shard_map/while/body/eval_jaxpr/dot_general | solution.py:26
  125.6 14.8 %fusion.41 = f32[32,32]{1,0:T(8,128)S(1)} fusion(bf16[3072,3072]{1,0:T(8,128)(2,1)} %convolution_convert_fusion.3, bf16[3072,3072]{1,0:T(8,128)(2,1)} %get-tuple-element.123, bf16[6,32,3072]{2,1,0:T(8,128)(2,1)S(1)} %get-tuple-element.125, s32[]{:T(128)} %get-tuple-element.111, bf16[6,32,3072]{2,1,0:T(8,128)(2,1)S(1)} %get-tuple-element.122, ...), kind=kOutput, calls=%fused_computation.8.clone.1 | convolution fusion | flops 648120320 | bytes 38148096 | tf_op jit(solution)/shard_map/while/body/eval_jaxpr/dot_general | solution.py:36
  140.3 0.1 broadcast_in_dim.31
  140.5 9.3 %convolution_convert_fusion.3 = bf16[3072,3072]{1,0:T(8,128)(2,1)} fusion(bf16[6,32,3072]{2,1,0:T(8,128)(2,1)S(1)} %get-tuple-element.125, s32[]{:T(128)} %get-tuple-element.111, bf16[6,32,3072]{2,1,0:T(8,128)(2,1)S(1)} %get-tuple-element.122, bf16[6,32,32]{2,1,0:T(8,128)(2,1)S(1)} %get-tuple-element.124), kind=kOutput, calls=%fused_computation.3.clone.1 | convolution fusion | flops 619806720 | bytes 19277312 | tf_op jit(solution)/shard_map/while/body/eval_jaxpr/dot_general | solution.py:26
  149.9 14.8 %fusion.41 = f32[32,32]{1,0:T(8,128)S(1)} fusion(bf16[3072,3072]{1,0:T(8,128)(2,1)} %convolution_convert_fusion.3, bf16[3072,3072]{1,0:T(8,128)(2,1)} %get-tuple-element.123, bf16[6,32,3072]{2,1,0:T(8,128)(2,1)S(1)} %get-tuple-element.125, s32[]{:T(128)} %get-tuple-element.111, bf16[6,32,3072]{2,1,0:T(8,128)(2,1)S(1)} %get-tuple-element.122, ...), kind=kOutput, calls=%fused_computation.8.clone.1 | convolution fusion | flops 648120320 | bytes 38148096 | tf_op jit(solution)/shard_map/while/body/eval_jaxpr/dot_general | solution.py:36
  164.6 0.1 broadcast_in_dim.31
  164.7 0.1 dynamic_update_slice.5
  164.8 9.3 %convolution_convert_fusion.3 = bf16[3072,3072]{1,0:T(8,128)(2,1)} fusion(bf16[6,32,3072]{2,1,0:T(8,128)(2,1)S(1)} %get-tuple-element.125, s32[]{:T(128)} %get-tuple-element.111, bf16[6,32,3072]{2,1,0:T(8,128)(2,1)S(1)} %get-tuple-element.122, bf16[6,32,32]{2,1,0:T(8,128)(2,1)S(1)} %get-tuple-element.124), kind=kOutput, calls=%fused_computation.3.clone.1 | convolution fusion | flops 619806720 | bytes 19277312 | tf_op jit(solution)/shard_map/while/body/eval_jaxpr/dot_general | solution.py:26
  174.2 14.8 %fusion.41 = f32[32,32]{1,0:T(8,128)S(1)} fusion(bf16[3072,3072]{1,0:T(8,128)(2,1)} %convolution_convert_fusion.3, bf16[3072,3072]{1,0:T(8,128)(2,1)} %get-tuple-element.123, bf16[6,32,3072]{2,1,0:T(8,128)(2,1)S(1)} %get-tuple-element.125, s32[]{:T(128)} %get-tuple-element.111, bf16[6,32,3072]{2,1,0:T(8,128)(2,1)S(1)} %get-tuple-element.122, ...), kind=kOutput, calls=%fused_computation.8.clone.1 | convolution fusion | flops 648120320 | bytes 38148096 | tf_op jit(solution)/shard_map/while/body/eval_jaxpr/dot_general | solution.py:36
  188.9 0.1 broadcast_in_dim.31
  189.1 9.3 %convolution_convert_fusion.3 = bf16[3072,3072]{1,0:T(8,128)(2,1)} fusion(bf16[6,32,3072]{2,1,0:T(8,128)(2,1)S(1)} %get-tuple-element.125, s32[]{:T(128)} %get-tuple-element.111, bf16[6,32,3072]{2,1,0:T(8,128)(2,1)S(1)} %get-tuple-element.122, bf16[6,32,32]{2,1,0:T(8,128)(2,1)S(1)} %get-tuple-element.124), kind=kOutput, calls=%fused_computation.3.clone.1 | convolution fusion | flops 619806720 | bytes 19277312 | tf_op jit(solution)/shard_map/while/body/eval_jaxpr/dot_general | solution.py:26
  198.5 14.8 %fusion.41 = f32[32,32]{1,0:T(8,128)S(1)} fusion(bf16[3072,3072]{1,0:T(8,128)(2,1)} %convolution_convert_fusion.3, bf16[3072,3072]{1,0:T(8,128)(2,1)} %get-tuple-element.123, bf16[6,32,3072]{2,1,0:T(8,128)(2,1)S(1)} %get-tuple-element.125, s32[]{:T(128)} %get-tuple-element.111, bf16[6,32,3072]{2,1,0:T(8,128)(2,1)S(1)} %get-tuple-element.122, ...), kind=kOutput, calls=%fused_computation.8.clone.1 | convolution fusion | flops 648120320 | bytes 38148096 | tf_op jit(solution)/shard_map/while/body/eval_jaxpr/dot_general | solution.py:36
  213.2 0.1 broadcast_in_dim.31
  213.4 59.4 %psum.7 = f32[6,1024]{1,0:T(8,128)S(1)} all-reduce(f32[6,1024]{1,0:T(8,128)S(1)} %get-tuple-element.42), channel_id=1, replica_groups=mesh['pair'=2,'grow'=4,'gcol'=4] {'grow','gcol'}, use_global_device_ids=true, to_apply=%region_2.3 | all-reduce | flops 6144 | bytes 49152 | tf_op jit(solution)/shard_map/psum | solution.py:41
  272.9 4.3 %all-gather = f32[2,6,64]{2,1,0:T(8,128)S(1)} all-gather(f32[1,6,64]{2,1,0:T(8,128)S(1)} %dynamic-slice_bitcast_fusion), channel_id=1, replica_groups=mesh['pair'=2,'grow'=4,'gcol'=4] {'pair'}, dimensions={0}, use_global_device_ids=true | all-gather | bytes 4608 | tf_op jit(solution)/shard_map/all_gather | solution.py:44
  277.2 0.6 gather_fusion
  277.8 0.7 broadcast_select_fusion
  (15 shorter events, 0.4 us)
Async XLA Ops:
  6.5 59.2 %all-gather.3.cloned.1.call-start = ((), (), s32[]{:S(2)}) async-start(), calls=%async_computation | async-start | bytes 5013504 | tf_op jit(solution)/shard_map/all_gather | solution.py:17
Sparse Core Ops, SparseCore 0:
  9.5 56.1 all-gather.2
where the time goes:
time: 286 us; the launch traced here: 285 us
  matrix products  145 us (51%)
  blocking collectives  63.7 us (22%)
  waiting for transfers between devices  56.2 us (20%)
  between operations  13.4 us (5%)
  other arithmetic  3.64 us (1%)
  local copies, waits for them, and re-layouts  3.44 us (1%)
    dot_general x6, matrix products, slot_term(): partial_sum = jnp.dot(left_panel, back, preferred_element_type=jnp.float32)  88.5 us
    psum x1, blocking collectives, local(): total = lax.psum(terms, ('grow', 'gcol'))  59.4 us
    dot_general x6, matrix products, slot_term(): lax.dot_general(left_panel, projected, (((0,), (0,)), ((), ())), preferre...  56.1 us
    all_gather x1, waiting for transfers between devices, local(): gathered = lax.all_gather(pair_panels, ('grow', 'gcol'), axis=2, tiled=True)  55.5 us
  transfers between devices with their start and end apart: 1, of which 1 were waited for; matrix products, arithmetic and copies ran while one was open for 1% of the time, Pallas kernels for 0%

commit v1 on v0

--- a/solution.py
+++ b/solution.py
@@ -38,7 +38,8 @@
         return (partial_sum * keep[:, None] * keep[None, :]).reshape(depth * depth)
 
     terms = lax.map(slot_term, (left, right, masked, live))
-    total = lax.psum(terms, ("grow", "gcol"))
+    parts = lax.all_gather(terms, ("grow", "gcol"))
+    total = jnp.sum(parts, axis=0)
     share = terms.shape[1] // lax.axis_size(("grow", "gcol"))
     reduced = lax.dynamic_slice_in_dim(total, lax.axis_index(("grow", "gcol")) * share, share, 1)
     every_row = lax.all_gather(reduced, "pair", axis=0, tiled=True)

time: 286 us -> 261 us (0.913)
  blocking collectives: 63.7 us -> 39 us
    psum x1 -> x0, blocking collectives: 59.4 us -> none  [local(): total = lax.psum(terms, ('grow', 'gcol'))]
    all_gather x0 -> x1, blocking collectives: none -> 34.6 us  [local(): parts = lax.all_gather(terms, ('grow', 'gcol'))]
where the time goes in v1:
time: 261 us
  matrix products  145 us (56%)
  waiting for transfers between devices  56.2 us (22%)
  blocking collectives  39 us (15%)
  between operations  13.4 us (5%)
  other arithmetic  3.69 us (1%)
  local copies, waits for them, and re-layouts  3.44 us (1%)
    dot_general x6, matrix products, slot_term(): partial_sum = jnp.dot(left_panel, back, preferred_element_type=jnp.float32)  88.5 us
    dot_general x6, matrix products, slot_term(): lax.dot_general(left_panel, projected, (((0,), (0,)), ((), ())), preferre...  56.1 us
    all_gather x1, waiting for transfers between devices, local(): gathered = lax.all_gather(pair_panels, ('grow', 'gcol'), axis=2, tiled=True)  55.5 us
    all_gather x1, blocking collectives, local(): parts = lax.all_gather(terms, ('grow', 'gcol'))  34.6 us
  transfers between devices with their start and end apart: 1, of which 1 were waited for; matrix products, arithmetic and copies ran while one was open for 1% of the time, Pallas kernels for 0%

profile of v1, /device:TPU:0, one launch (start us, length us, event | category | flops | bytes accessed | tf_op | source)
XLA Modules:
  0.0 260.6 jit_solution(880381371381873054)
XLA Ops:
  6.5 0.7 all-gather.5.cloned.1.call-update
  7.3 0.7 compare_select_fusion
  8.0 0.7 compare_and_fusion
  8.6 0.7 fusion.27
  9.3 0.9 multiply_multiply_fusion
  10.2 55.5 %all-gather.5.cloned.1.call-done = bf16[6,32,12288]{2,1,0:T(8,128)(2,1)} async-done(((bf16[6,32,768]{2,1,0:T(8,128)(2,1)}), bf16[6,32,12288]{2,1,0:T(8,128)(2,1)}) %all-gather.5.cloned.1.call-update) | async-done | bytes 4718608 | tf_op jit(solution)/shard_map/all_gather | solution.py:17
  65.8 1.9 constant_dynamic-slice_fusion.1
  67.6 145.8 %while.10 = (s32[]{:T(128)}, f32[6,1024]{1,0:T(8,128)S(1)}, bf16[6,32,3072]{2,1,0:T(8,128)(2,1)S(1)}, bf16[3072,3072]{1,0:T(8,128)(2,1)}, bf16[6,32,32]{2,1,0:T(...) while((s32[]{:T(128)}, f32[6,1024]{1,0:T(8,128)S(1)}, ...), condition=%wide.region_1.2_spmd, body=%wide.region_0.1_spmd.sunk | while | flops 1267927040 | bytes 57442084 | solution.py:40
  67.6 9.3 %convolution_convert_fusion.3 = bf16[3072,3072]{1,0:T(8,128)(2,1)} fusion(bf16[6,32,3072]{2,1,0:T(8,128)(2,1)S(1)} %get-tuple-element.125, s32[]{:T(128)} %get-tuple-element.111, bf16[6,32,3072]{2,1,0:T(8,128)(2,1)S(1)} %get-tuple-element.122, bf16[6,32,32]{2,1,0:T(8,128)(2,1)S(1)} %get-tuple-element.124), kind=kOutput, calls=%fused_computation.3.clone.1 | convolution fusion | flops 619806720 | bytes 19277312 | tf_op jit(solution)/shard_map/while/body/eval_jaxpr/dot_general | solution.py:26
  77.0 14.8 %fusion.41 = f32[32,32]{1,0:T(8,128)S(1)} fusion(bf16[3072,3072]{1,0:T(8,128)(2,1)} %convolution_convert_fusion.3, bf16[3072,3072]{1,0:T(8,128)(2,1)} %get-tuple-element.123, bf16[6,32,3072]{2,1,0:T(8,128)(2,1)S(1)} %get-tuple-element.125, s32[]{:T(128)} %get-tuple-element.111, bf16[6,32,3072]{2,1,0:T(8,128)(2,1)S(1)} %get-tuple-element.122, ...), kind=kOutput, calls=%fused_computation.8.clone.1 | convolution fusion | flops 648120320 | bytes 38148096 | tf_op jit(solution)/shard_map/while/body/eval_jaxpr/dot_general | solution.py:36
  91.8 0.1 broadcast_in_dim.31
  91.8 0.1 dynamic_update_slice.5
  91.9 9.3 %convolution_convert_fusion.3 = bf16[3072,3072]{1,0:T(8,128)(2,1)} fusion(bf16[6,32,3072]{2,1,0:T(8,128)(2,1)S(1)} %get-tuple-element.125, s32[]{:T(128)} %get-tuple-element.111, bf16[6,32,3072]{2,1,0:T(8,128)(2,1)S(1)} %get-tuple-element.122, bf16[6,32,32]{2,1,0:T(8,128)(2,1)S(1)} %get-tuple-element.124), kind=kOutput, calls=%fused_computation.3.clone.1 | convolution fusion | flops 619806720 | bytes 19277312 | tf_op jit(solution)/shard_map/while/body/eval_jaxpr/dot_general | solution.py:26
  101.3 14.8 %fusion.41 = f32[32,32]{1,0:T(8,128)S(1)} fusion(bf16[3072,3072]{1,0:T(8,128)(2,1)} %convolution_convert_fusion.3, bf16[3072,3072]{1,0:T(8,128)(2,1)} %get-tuple-element.123, bf16[6,32,3072]{2,1,0:T(8,128)(2,1)S(1)} %get-tuple-element.125, s32[]{:T(128)} %get-tuple-element.111, bf16[6,32,3072]{2,1,0:T(8,128)(2,1)S(1)} %get-tuple-element.122, ...), kind=kOutput, calls=%fused_computation.8.clone.1 | convolution fusion | flops 648120320 | bytes 38148096 | tf_op jit(solution)/shard_map/while/body/eval_jaxpr/dot_general | solution.py:36
  116.1 0.1 broadcast_in_dim.31
  116.2 9.3 %convolution_convert_fusion.3 = bf16[3072,3072]{1,0:T(8,128)(2,1)} fusion(bf16[6,32,3072]{2,1,0:T(8,128)(2,1)S(1)} %get-tuple-element.125, s32[]{:T(128)} %get-tuple-element.111, bf16[6,32,3072]{2,1,0:T(8,128)(2,1)S(1)} %get-tuple-element.122, bf16[6,32,32]{2,1,0:T(8,128)(2,1)S(1)} %get-tuple-element.124), kind=kOutput, calls=%fused_computation.3.clone.1 | convolution fusion | flops 619806720 | bytes 19277312 | tf_op jit(solution)/shard_map/while/body/eval_jaxpr/dot_general | solution.py:26
  125.6 14.8 %fusion.41 = f32[32,32]{1,0:T(8,128)S(1)} fusion(bf16[3072,3072]{1,0:T(8,128)(2,1)} %convolution_convert_fusion.3, bf16[3072,3072]{1,0:T(8,128)(2,1)} %get-tuple-element.123, bf16[6,32,3072]{2,1,0:T(8,128)(2,1)S(1)} %get-tuple-element.125, s32[]{:T(128)} %get-tuple-element.111, bf16[6,32,3072]{2,1,0:T(8,128)(2,1)S(1)} %get-tuple-element.122, ...), kind=kOutput, calls=%fused_computation.8.clone.1 | convolution fusion | flops 648120320 | bytes 38148096 | tf_op jit(solution)/shard_map/while/body/eval_jaxpr/dot_general | solution.py:36
  140.3 0.1 broadcast_in_dim.31
  140.5 9.3 %convolution_convert_fusion.3 = bf16[3072,3072]{1,0:T(8,128)(2,1)} fusion(bf16[6,32,3072]{2,1,0:T(8,128)(2,1)S(1)} %get-tuple-element.125, s32[]{:T(128)} %get-tuple-element.111, bf16[6,32,3072]{2,1,0:T(8,128)(2,1)S(1)} %get-tuple-element.122, bf16[6,32,32]{2,1,0:T(8,128)(2,1)S(1)} %get-tuple-element.124), kind=kOutput, calls=%fused_computation.3.clone.1 | convolution fusion | flops 619806720 | bytes 19277312 | tf_op jit(solution)/shard_map/while/body/eval_jaxpr/dot_general | solution.py:26
  149.9 14.8 %fusion.41 = f32[32,32]{1,0:T(8,128)S(1)} fusion(bf16[3072,3072]{1,0:T(8,128)(2,1)} %convolution_convert_fusion.3, bf16[3072,3072]{1,0:T(8,128)(2,1)} %get-tuple-element.123, bf16[6,32,3072]{2,1,0:T(8,128)(2,1)S(1)} %get-tuple-element.125, s32[]{:T(128)} %get-tuple-element.111, bf16[6,32,3072]{2,1,0:T(8,128)(2,1)S(1)} %get-tuple-element.122, ...), kind=kOutput, calls=%fused_computation.8.clone.1 | convolution fusion | flops 648120320 | bytes 38148096 | tf_op jit(solution)/shard_map/while/body/eval_jaxpr/dot_general | solution.py:36
  164.6 0.1 broadcast_in_dim.31
  164.7 0.1 dynamic_update_slice.5
  164.8 9.3 %convolution_convert_fusion.3 = bf16[3072,3072]{1,0:T(8,128)(2,1)} fusion(bf16[6,32,3072]{2,1,0:T(8,128)(2,1)S(1)} %get-tuple-element.125, s32[]{:T(128)} %get-tuple-element.111, bf16[6,32,3072]{2,1,0:T(8,128)(2,1)S(1)} %get-tuple-element.122, bf16[6,32,32]{2,1,0:T(8,128)(2,1)S(1)} %get-tuple-element.124), kind=kOutput, calls=%fused_computation.3.clone.1 | convolution fusion | flops 619806720 | bytes 19277312 | tf_op jit(solution)/shard_map/while/body/eval_jaxpr/dot_general | solution.py:26
  174.2 14.8 %fusion.41 = f32[32,32]{1,0:T(8,128)S(1)} fusion(bf16[3072,3072]{1,0:T(8,128)(2,1)} %convolution_convert_fusion.3, bf16[3072,3072]{1,0:T(8,128)(2,1)} %get-tuple-element.123, bf16[6,32,3072]{2,1,0:T(8,128)(2,1)S(1)} %get-tuple-element.125, s32[]{:T(128)} %get-tuple-element.111, bf16[6,32,3072]{2,1,0:T(8,128)(2,1)S(1)} %get-tuple-element.122, ...), kind=kOutput, calls=%fused_computation.8.clone.1 | convolution fusion | flops 648120320 | bytes 38148096 | tf_op jit(solution)/shard_map/while/body/eval_jaxpr/dot_general | solution.py:36
  188.9 0.1 broadcast_in_dim.31
  189.1 9.3 %convolution_convert_fusion.3 = bf16[3072,3072]{1,0:T(8,128)(2,1)} fusion(bf16[6,32,3072]{2,1,0:T(8,128)(2,1)S(1)} %get-tuple-element.125, s32[]{:T(128)} %get-tuple-element.111, bf16[6,32,3072]{2,1,0:T(8,128)(2,1)S(1)} %get-tuple-element.122, bf16[6,32,32]{2,1,0:T(8,128)(2,1)S(1)} %get-tuple-element.124), kind=kOutput, calls=%fused_computation.3.clone.1 | convolution fusion | flops 619806720 | bytes 19277312 | tf_op jit(solution)/shard_map/while/body/eval_jaxpr/dot_general | solution.py:26
  198.5 14.8 %fusion.41 = f32[32,32]{1,0:T(8,128)S(1)} fusion(bf16[3072,3072]{1,0:T(8,128)(2,1)} %convolution_convert_fusion.3, bf16[3072,3072]{1,0:T(8,128)(2,1)} %get-tuple-element.123, bf16[6,32,3072]{2,1,0:T(8,128)(2,1)S(1)} %get-tuple-element.125, s32[]{:T(128)} %get-tuple-element.111, bf16[6,32,3072]{2,1,0:T(8,128)(2,1)S(1)} %get-tuple-element.122, ...), kind=kOutput, calls=%fused_computation.8.clone.1 | convolution fusion | flops 648120320 | bytes 38148096 | tf_op jit(solution)/shard_map/while/body/eval_jaxpr/dot_general | solution.py:36
  213.2 0.1 broadcast_in_dim.31
  213.4 34.6 %all-gather.1 = f32[16,6,1024]{2,1,0:T(8,128)S(1)} all-gather(f32[1,6,1024]{2,1,0:T(8,128)S(1)} %bitcast.36), channel_id=2, replica_groups=mesh['pair'=2,'grow'=4,'gcol'=4] {'grow','gcol'}, dimensions={0}, use_global_device_ids=true | all-gather | bytes 417792 | tf_op jit(solution)/shard_map/all_gather | solution.py:41
  248.1 4.3 %all-gather.2 = f32[2,6,64]{2,1,0:T(8,128)S(1)} all-gather(f32[1,6,64]{2,1,0:T(8,128)S(1)} %dynamic-slice_bitcast_fusion), channel_id=1, replica_groups=mesh['pair'=2,'grow'=4,'gcol'=4] {'pair'}, dimensions={0}, use_global_device_ids=true | all-gather | bytes 4608 | tf_op jit(solution)/shard_map/all_gather | solution.py:45
  252.5 0.6 gather_fusion
  253.0 0.7 broadcast_select_fusion
  (16 shorter events, 0.5 us)
Async XLA Ops:
  6.5 59.2 %all-gather.5.cloned.1.call-start = ((), (), s32[]{:S(2)}) async-start(), calls=%async_computation | async-start | bytes 5013504 | tf_op jit(solution)/shard_map/all_gather | solution.py:17
Sparse Core Ops, SparseCore 0:
  9.5 56.1 all-gather.4
